TPU v7x, 32 devices: a whole 2x2x4 slice. The times are simulated.
32 devices in a mesh: branch: 8 (over y, x, core), mode: 4 (over z).
Axes of the slice: x: 2, y: 2, z: 4, core: 2. Of those that a mesh axis runs over, the one named last changes fastest.
Arguments:
- stem: float32 [2, 8, 512, 4, 512], P(None, 'branch', None, 'mode'), may hold values from -6 to 6
- left_factors: bfloat16 [2, 2, 8, 512, 512], P(None, None, 'branch', 'mode'), may hold values from -0.1875 to 0.1875
- right_factors: bfloat16 [2, 2, 8, 512, 512], P(None, None, 'branch', 'mode'), may hold values from -0.1875 to 0.1875
- owners: int32 [2], replicated, may hold values from 0 to 7
Outputs:
- contracted: float32 [2, 8, 512, 4, 512], P(None, 'branch', None, 'mode')
All inputs are finite; a program needn't handle non-finite values.
Results may differ from a plain program's by a relative error of at most 0.0003.
Values may be sent and summed in bfloat16 or wider, within the bound.
No kernel may reach another device: no remote copies, remote signals or barrier semaphores. Data moves between devices by JAX's collectives and lax.ppermute only.
A program may use at most 64 MiB of HBM per device.

v0:
```python
import jax
import jax.numpy as jnp
from jax import lax
from jax.sharding import PartitionSpec as P


def spread(block, axis, holder):
    block = jnp.where(lax.axis_index(axis) == holder, block, jnp.zeros_like(block))
    return lax.psum(block, axis)


def complex_apply(field_re, field_im, branch):
    high = lax.Precision.HIGHEST
    real_part = jnp.dot(field_re, branch[0], precision=high) - jnp.dot(
        field_im, branch[1], precision=high
    )
    imag_part = jnp.dot(field_re, branch[1], precision=high) + jnp.dot(
        field_im, branch[0], precision=high
    )
    return (real_part, imag_part)


def shards(stem, left_factors, right_factors, owners):
    width = stem.shape[4]

    def form_branch(which):
        left = left_factors[which, :, 0]
        right = right_factors[which]
        piece = lax.all_gather(right, "mode", axis=2, tiled=True)
        real_part = jnp.dot(left[0], piece[0, 0], preferred_element_type=jnp.float32) - jnp.dot(
            left[1], piece[1, 0], preferred_element_type=jnp.float32
        )
        imag_part = jnp.dot(left[0], piece[1, 0], preferred_element_type=jnp.float32) + jnp.dot(
            left[1], piece[0, 0], preferred_element_type=jnp.float32
        )
        formed = jnp.stack([real_part, imag_part])
        holder = owners[which]
        received = spread(formed, "branch", holder)
        return lax.all_gather(received, "mode", axis=1, tiled=True)

    first_branch = form_branch(0)
    second_branch = form_branch(1)
    real_one, imag_one = complex_apply(stem[0, 0, :, 0, :], stem[1, 0, :, 0, :], first_branch)
    outgoing = jnp.stack([real_one, imag_one])[:, None, :, None, :]
    arrived = lax.all_to_all(outgoing, "mode", split_axis=4, concat_axis=3, tiled=True)
    count = arrived.shape[2]
    merged = arrived.reshape(2, count, width)
    real_two, imag_two = complex_apply(merged[0], merged[1], second_branch)
    return jnp.stack([real_two, imag_two])[:, None, :, None, :]


def solution(mesh):
    placed = (
        P(None, "branch", None, "mode", None),
        P(None, None, "branch", "mode", None),
        P(None, None, "branch", "mode", None),
        P(),
    )
    return jax.shard_map(
        shards,
        mesh=mesh,
        in_specs=placed,
        out_specs=P(None, "branch", None, "mode", None),
        check_vma=False,
    )
```

profile of v0, /device:TPU:0, one launch (start us, length us, event | category | flops | bytes accessed | tf_op | source)
XLA Modules:
  0.0 303.5 jit_solution(10032876281530875387)
XLA Ops:
  6.5 1.9 fusion.50
  9.3 1.3 fusion.51
  11.9 27.8 %all-gather.11.cloned.1.call-done = bf16[1,2,1,512,512]{4,3,2,1,0:T(8,128)(2,1)} async-done(((bf16[1,2,1,128,512]{4,3,2,1,0:T(8,128)(2,1)}), bf16[1,2,1,512,512]{4,3,2,1,0:T(8,128)(2,1)}) %all-gather.11.cloned.1.call-update) | async-done | bytes 1048592 | tf_op jit(solution)/shard_map/all_gather | solution.py:29
  39.6 1.4 fusion.29
  41.1 1.3 fusion.6
  43.7 24.9 %all-gather.13.cloned.1.call-done = bf16[1,2,1,512,512]{4,3,2,1,0:T(8,128)(2,1)} async-done(((bf16[1,2,1,128,512]{4,3,2,1,0:T(8,128)(2,1)}), bf16[1,2,1,512,512]{4,3,2,1,0:T(8,128)(2,1)}) %all-gather.13.cloned.1.call-update) | async-done | bytes 1048592 | tf_op jit(solution)/shard_map/all_gather | solution.py:29
  68.6 1.4 fusion.30
  70.0 1.3 fusion.31
  72.7 56.3 %all-reduce.3.cloned.1.call-done = (f32[2,128,512]{2,1,0:T(8,128)}, f32[2,128,512]{2,1,0:T(8,128)}) async-done(((f32[2,128,512]{2,1,0:T(8,128)}, f32[2,128,512]{2,1,0:T(8,128)}), (f32[2,128,512]{2,1,0:T(8,128)}, f32[2,128,512]{2,1,0:T(8,128)})) %all-reduce.3.cloned.1.call-update) | async-done | bytes 1048592 | tf_op jit(solution)/shard_map/psum | solution.py:9
  129.0 3.0 fusion.49
  131.9 43.4 %all-gather.7.cloned.1.call-done = f32[2,512,512]{2,1,0:T(8,128)} async-done(((f32[2,128,512]{2,1,0:T(8,128)}), f32[2,512,512]{2,1,0:T(8,128)}) %all-gather.7.cloned.1.call-update) | async-done | bytes 2097168 | tf_op jit(solution)/shard_map/all_gather | solution.py:39
  175.3 4.8 %fusion.18 = f32[512,512]{1,0:T(8,128)S(1)} fusion(f32[2,512,512]{2,1,0:T(8,128)} %all-gather.7.cloned.1.call-done, f32[1,1,512,1,512]{4,3,2,1,0:T(1,128)S(1)} %get-tuple-element.10), kind=kOutput, calls=%fused_computation.32 | convolution fusion | flops 1610612736 | bytes 3145728 | tf_op jit(solution)/shard_map/dot_general | solution.py:14
  180.2 3.5 %fusion.16 = f32[512,512]{1,0:T(8,128)S(1)} fusion(f32[2,512,512]{2,1,0:T(8,128)S(1)} %copy-done.1, f32[1,1,512,1,512]{4,3,2,1,0:T(1,128)S(1)} %get-tuple-element.10), kind=kOutput, calls=%fused_computation.30 | convolution fusion | flops 1610612736 | bytes 3145728 | tf_op jit(solution)/shard_map/dot_general | solution.py:17
  183.7 3.5 %fusion.3 = f32[1,512,512]{1,2,0:T(8,128)S(1)} fusion(f32[512,512]{1,0:T(8,128)S(1)} %fusion.18, f32[2,512,512]{2,1,0:T(8,128)S(1)} %copy-done.1, f32[1,1,512,1,512]{4,3,2,1,0:T(1,128)S(1)} %get-tuple-element.9), kind=kOutput, calls=%fused_computation.9 | convolution fusion | flops 1610874880 | bytes 4194304 | tf_op jit(solution)/shard_map/dot_general | solution.py:14
  187.1 3.7 %fusion.2 = f32[1,512,512]{1,2,0:T(8,128)S(1)} fusion(f32[512,512]{1,0:T(8,128)S(1)} %fusion.16, f32[2,512,512]{2,1,0:T(8,128)S(1)} %copy-done.1, f32[1,1,512,1,512]{4,3,2,1,0:T(1,128)S(1)} %get-tuple-element.9), kind=kOutput, calls=%fused_computation.7 | convolution fusion | flops 1610874880 | bytes 4194304 | tf_op jit(solution)/shard_map/dot_general | solution.py:17
  191.0 2.9 copy.6
  193.9 4.4 %all-to-all-start = ((f32[2,1,512,1,512]{2,0,3,1,4:T(2,128)}), f32[2,1,512,1,512]{2,0,3,1,4:T(2,128)}, u32[]{:S(2)}, u32[]{:S(2)}) async-start(f32[2,1,512,1,512]{2,0,3,1,4:T(2,128)} %copy.6), calls=%async_computation | async-start | bytes 4194304 | tf_op jit(solution)/shard_map/all_to_all | solution.py:45
  199.0 81.5 %all-to-all-done = f32[2,1,512,1,512]{2,0,3,1,4:T(2,128)} async-done(((f32[2,1,512,1,512]{2,0,3,1,4:T(2,128)}), f32[2,1,512,1,512]{2,0,3,1,4:T(2,128)}, u32[]{:S(2)}, u32[]{:S(2)}) %all-to-all-start) | async-done | bytes 2097184 | tf_op jit(solution)/shard_map/all_to_all | solution.py:45
  280.5 4.0 %fusion.48 = (f32[1,1,512,1,512]{2,0,3,1,4:T(1,128)S(1)}, f32[1,1,512,1,512]{2,0,3,1,4:T(1,128)S(1)}) fusion(f32[2,1,512,1,512]{2,0,3,1,4:T(2,128)} %all-to-all-done), kind=kLoop, calls=%fused_computation.68 | loop fusion | bytes 4194304 | tf_op jit(solution)/shard_map/slice | solution.py:48
  284.5 3.2 %fusion.12 = f32[512,512]{1,0:T(8,128)S(1)} fusion(f32[2,512,512]{2,1,0:T(8,128)} %all-gather.9.cloned.1.call-done, f32[1,1,512,1,512]{2,0,3,1,4:T(1,128)S(1)} %get-tuple-element.8), kind=kOutput, calls=%fused_computation.26 | convolution fusion | flops 1610612736 | bytes 3145728 | tf_op jit(solution)/shard_map/dot_general | solution.py:14
  287.8 1.9 fusion.10
  289.6 1.9 fusion.1
  291.5 1.9 fusion
  293.5 3.5 %copy.7 = f32[2,1,512,1,512]{4,3,2,1,0:T(1,128)} copy(f32[2,1,512,1,512]{4,2,0,3,1:T(8,128)S(1)} %maximum_bitcast_fusion.1) | data formatting | bytes 4194304 | tf_op jit(solution)/shard_map/broadcast_in_dim | solution.py:49
  (29 shorter events, 4.4 us)
Async XLA Ops:
  6.5 34.5 %copy-start.4 = (bf16[2,2,1,128,512]{4,3,2,1,0:T(8,128)(2,1)S(1)}, bf16[2,2,1,128,512]{4,3,2,1,0:T(8,128)(2,1)}, u32[]{:S(2)}) copy-start(bf16[2,2,1,128,512]{4,3,2,1,0:T(8,128)(2,1)} %param.5) | copy-start | bytes 1572868
  6.5 33.1 %all-gather.11.cloned.1.call-start = ((), (), s32[]{:S(2)}) async-start(), calls=%async_computation.3 | async-start | bytes 1310720 | tf_op jit(solution)/shard_map/all_gather | solution.py:29
  8.5 60.2 %all-gather.13.cloned.1.call-start = ((), (), s32[]{:S(2)}) async-start(), calls=%async_computation.4 | async-start | bytes 1310720 | tf_op jit(solution)/shard_map/all_gather | solution.py:29
  9.2 119.7 %all-reduce.3.cloned.1.call-start = ((), (), s32[]{:S(2)}) async-start(), calls=%async_computation.5 | async-start | bytes 2097152 | tf_op jit(solution)/shard_map/psum | solution.py:9
  39.6 2.7 copy-start.3
  68.6 2.6 copy-start.2
  72.6 102.7 %all-gather.7.cloned.1.call-start = ((), (), s32[]{:S(2)}) async-start(), calls=%async_computation.1 | async-start | bytes 2621440 | tf_op jit(solution)/shard_map/all_gather | solution.py:39
  175.3 4.9 %copy-start.1 = (f32[2,512,512]{2,1,0:T(8,128)S(1)}, f32[2,512,512]{2,1,0:T(8,128)}, u32[]{:S(2)}) copy-start(f32[2,512,512]{2,1,0:T(8,128)} %all-gather.7.cloned.1.call-done) | copy-start | bytes 6291460
  193.9 86.5 %all-to-all-start = ((f32[2,1,512,1,512]{2,0,3,1,4:T(2,128)}), f32[2,1,512,1,512]{2,0,3,1,4:T(2,128)}, u32[]{:S(2)}, u32[]{:S(2)}) async-start(f32[2,1,512,1,512]{2,0,3,1,4:T(2,128)} %copy.6), calls=%async_computation | async-start | bytes 4194304 | tf_op jit(solution)/shard_map/all_to_all | solution.py:45
  198.4 86.1 %all-gather.9.cloned.1.call-start = ((), (), s32[]{:S(2)}) async-start(), calls=%async_computation.2 | async-start | bytes 2621440 | tf_op jit(solution)/shard_map/all_gather | solution.py:39
  284.5 3.2 %copy-start = (f32[2,512,512]{2,1,0:T(8,128)S(1)}, f32[2,512,512]{2,1,0:T(8,128)}, u32[]{:S(2)}) copy-start(f32[2,512,512]{2,1,0:T(8,128)} %all-gather.9.cloned.1.call-done) | copy-start | bytes 6291460
Sparse Core Ops, SparseCore 0:
  8.9 30.6 all-gather.10
  41.2 27.3 all-gather.12
  72.7 56.1 all-reduce.2
  130.4 44.9 all-gather.6
  200.4 74.5 all-gather.8
where the time goes:
time: 304 us
  waiting for transfers between devices  235 us (77%)
  matrix products  30.5 us (10%)
  local copies, waits for them, and re-layouts  16.7 us (5%)
  between operations  14.6 us (5%)
  starting transfers between devices  4.61 us (2%)
    all_to_all x1, waiting for transfers between devices, shards(): lax.all_to_all(outgoing, 'mode', split_axis=4, concat_axis=3, tiled=True)  81.5 us
    psum x1, waiting for transfers between devices, spread(): return lax.psum(block, axis)  56.3 us
    all_gather x2, waiting for transfers between devices, form_branch(): piece = lax.all_gather(right, 'mode', axis=2, tiled=True)  52.7 us
    all_gather x2, waiting for transfers between devices, form_branch(): return lax.all_gather(received, 'mode', axis=1, tiled=True)  43.4 us
    dot_general x2, matrix products, complex_apply(): jnp.dot(field_re, branch[0], precision=high)  8.07 us
  transfers between devices with their start and end apart: 6, of which 5 were waited for; matrix products, arithmetic and copies ran while one was open for 4% of the time, Pallas kernels for 0%

commit v1 on v0

--- a/solution.py
+++ b/solution.py
@@ -2,6 +2,11 @@
 import jax.numpy as jnp
 from jax import lax
 from jax.sharding import PartitionSpec as P
+
+
+def gather_over(block, axis, d):
+    outgoing = jnp.stack([block] * lax.axis_size(axis))
+    return jnp.concatenate(lax.all_to_all(outgoing, axis, 0, 0), axis=d)
 
 
 def spread(block, axis, holder):
@@ -36,7 +41,7 @@
         formed = jnp.stack([real_part, imag_part])
         holder = owners[which]
         received = spread(formed, "branch", holder)
-        return lax.all_gather(received, "mode", axis=1, tiled=True)
+        return gather_over(received, "mode", 1)
 
     first_branch = form_branch(0)
     second_branch = form_branch(1)

time: 304 us -> 310 us (1.020)
  waiting for transfers between devices: 235 us -> 182 us
  blocking collectives: 0 us -> 52 us
  local copies, waits for them, and re-layouts: 16.7 us -> 23.1 us
  starting transfers between devices: 4.61 us -> 8.15 us
    all_to_all x0 -> x1, blocking collectives: none -> 52 us  [gather_over(): return jnp.concatenate(lax.all_to_all(outgoing, axis, 0, 0), axis=d)]
    all_gather x2 -> x0, waiting for transfers between devices: 43.4 us -> none  [form_branch(): return lax.all_gather(received, 'mode', axis=1, tiled=True)]
    all_to_all x1, waiting for transfers between devices: 81.5 us -> 46 us  [shards(): lax.all_to_all(outgoing, 'mode', split_axis=4, concat_axis=3, tiled=True)]
    all_to_all x0 -> x1, waiting for transfers between devices: none -> 26.3 us  [gather_over(): return jnp.concatenate(lax.all_to_all(outgoing, axis, 0, 0), axis=d)]
    all_to_all x0 -> x1, starting transfers between devices: none -> 3.61 us  [gather_over(): return jnp.concatenate(lax.all_to_all(outgoing, axis, 0, 0), axis=d)]
  transfers between devices with their start and end apart: 6 -> 5, of which waited for: 5 -> 5; matrix products, arithmetic and copies ran while one was open for 4% -> 9% of each run, Pallas kernels for 0% -> 0%
where the time goes in v1:
time: 310 us
  waiting for transfers between devices  182 us (59%)
  blocking collectives  52 us (17%)
  matrix products  28.1 us (9%)
  local copies, waits for them, and re-layouts  23.1 us (7%)
  between operations  14.6 us (5%)
  starting transfers between devices  8.15 us (3%)
    psum x1, waiting for transfers between devices, spread(): return lax.psum(block, axis)  56.3 us
    all_gather x2, waiting for transfers between devices, form_branch(): piece = lax.all_gather(right, 'mode', axis=2, tiled=True)  52.7 us
    all_to_all x1, blocking collectives, gather_over(): return jnp.concatenate(lax.all_to_all(outgoing, axis, 0, 0), axis=d)  52 us
    all_to_all x1, waiting for transfers between devices, shards(): lax.all_to_all(outgoing, 'mode', split_axis=4, concat_axis=3, tiled=True)  46 us
    all_to_all x1, waiting for transfers between devices, gather_over(): return jnp.concatenate(lax.all_to_all(outgoing, axis, 0, 0), axis=d)  26.3 us
  transfers between devices with their start and end apart: 5, of which 5 were waited for; matrix products, arithmetic and copies ran while one was open for 9% of the time, Pallas kernels for 0%

profile of v1, /device:TPU:0, one launch (start us, length us, event | category | flops | bytes accessed | tf_op | source)
XLA Modules:
  0.0 309.9 jit_solution(14430087132913416663)
XLA Ops:
  6.5 1.9 fusion.52
  11.9 27.7 %all-gather.5.cloned.1.call-done = bf16[1,2,1,512,512]{4,3,2,1,0:T(8,128)(2,1)} async-done(((bf16[1,2,1,128,512]{4,3,2,1,0:T(8,128)(2,1)}), bf16[1,2,1,512,512]{4,3,2,1,0:T(8,128)(2,1)}) %all-gather.5.cloned.1.call-update) | async-done | bytes 1048592 | tf_op jit(solution)/shard_map/all_gather | solution.py:34
  39.6 1.4 fusion.29
  43.7 25.0 %all-gather.7.cloned.1.call-done = bf16[1,2,1,512,512]{4,3,2,1,0:T(8,128)(2,1)} async-done(((bf16[1,2,1,128,512]{4,3,2,1,0:T(8,128)(2,1)}), bf16[1,2,1,512,512]{4,3,2,1,0:T(8,128)(2,1)}) %all-gather.7.cloned.1.call-update) | async-done | bytes 1048592 | tf_op jit(solution)/shard_map/all_gather | solution.py:34
  72.6 56.3 %all-reduce.3.cloned.1.call-done = (f32[2,128,512]{2,1,0:T(8,128)}, f32[2,128,512]{2,1,0:T(8,128)}) async-done(((f32[2,128,512]{2,1,0:T(8,128)}, f32[2,128,512]{2,1,0:T(8,128)}), (f32[2,128,512]{2,1,0:T(8,128)}, f32[2,128,512]{2,1,0:T(8,128)})) %all-reduce.3.cloned.1.call-update) | async-done | bytes 1048592 | tf_op jit(solution)/shard_map/psum | solution.py:14
  130.2 52.0 %all_to_all.19 = f32[4,2,128,512]{3,2,1,0:T(8,128)} all-to-all(f32[4,2,128,512]{3,2,1,0:T(8,128)S(1)} %stack.53), channel_id=1, replica_groups=mesh['branch'=8,'mode'=4] {'mode'}, dimensions={0} | all-to-all | bytes 4194304 | tf_op jit(solution)/shard_map/all_to_all | solution.py:9
  182.2 1.6 stack.60
  183.8 3.6 %all-to-all-start.2 = ((f32[4,2,128,512]{3,2,1,0:T(8,128)}), f32[4,2,128,512]{3,2,1,0:T(8,128)S(1)}, u32[]{:S(2)}, u32[]{:S(2)}) async-start(f32[4,2,128,512]{3,2,1,0:T(8,128)} %stack.60), calls=%async_computation.2 | async-start | bytes 4194304 | tf_op jit(solution)/shard_map/all_to_all | solution.py:9
  187.4 3.1 %fusion.50 = (f32[1,1,512,1,512]{4,3,2,1,0:T(1,128)S(1)}, f32[1,1,512,1,512]{4,3,2,1,0:T(1,128)S(1)}) fusion(f32[2,1,512,1,512]{4,3,2,1,0:T(1,128)} %param.4), kind=kLoop, calls=%fused_computation.66 | loop fusion | bytes 4194304 | tf_op jit(solution)/shard_map/slice | solution.py:48
  190.8 3.6 %fusion.18 = f32[512,512]{1,0:T(8,128)S(1)} fusion(f32[512,512]{1,0:T(8,128)S(1)} %bitcast.100, f32[1,1,512,1,512]{4,3,2,1,0:T(1,128)S(1)} %get-tuple-element.12), kind=kOutput, calls=%fused_computation.28 | convolution fusion | flops 1610612736 | bytes 3145728 | tf_op jit(solution)/shard_map/dot_general | solution.py:19
  194.3 3.6 %fusion.3 = f32[1,512,512]{1,2,0:T(8,128)S(1)} fusion(f32[512,512]{1,0:T(8,128)S(1)} %fusion.18, f32[512,512]{1,0:T(8,128)S(1)} %bitcast.102, f32[1,1,512,1,512]{4,3,2,1,0:T(1,128)S(1)} %get-tuple-element.11), kind=kOutput, calls=%fused_computation.9 | convolution fusion | flops 1610874880 | bytes 4194304 | tf_op jit(solution)/shard_map/dot_general | solution.py:19
  197.9 3.6 %fusion.16 = f32[512,512]{1,0:T(8,128)S(1)} fusion(f32[512,512]{1,0:T(8,128)S(1)} %bitcast.103, f32[1,1,512,1,512]{4,3,2,1,0:T(1,128)S(1)} %get-tuple-element.12), kind=kOutput, calls=%fused_computation.26 | convolution fusion | flops 1610612736 | bytes 3145728 | tf_op jit(solution)/shard_map/dot_general | solution.py:22
  201.5 3.7 %fusion.2 = f32[1,512,512]{1,2,0:T(8,128)S(1)} fusion(f32[512,512]{1,0:T(8,128)S(1)} %fusion.16, f32[512,512]{1,0:T(8,128)S(1)} %bitcast.101, f32[1,1,512,1,512]{4,3,2,1,0:T(1,128)S(1)} %get-tuple-element.11), kind=kOutput, calls=%fused_computation.7 | convolution fusion | flops 1610874880 | bytes 4194304 | tf_op jit(solution)/shard_map/dot_general | solution.py:22
  205.4 2.9 copy.6
  208.3 26.3 %all-to-all-done.2 = f32[4,2,128,512]{3,2,1,0:T(8,128)S(1)} async-done(((f32[4,2,128,512]{3,2,1,0:T(8,128)}), f32[4,2,128,512]{3,2,1,0:T(8,128)S(1)}, u32[]{:S(2)}, u32[]{:S(2)}) %all-to-all-start.2) | async-done | bytes 2097184 | tf_op jit(solution)/shard_map/all_to_all | solution.py:9
  235.9 4.5 %all-to-all-start.1 = ((f32[2,1,512,1,512]{2,0,3,1,4:T(2,128)}), f32[2,1,512,1,512]{2,0,3,1,4:T(2,128)}, u32[]{:S(2)}, u32[]{:S(2)}) async-start(f32[2,1,512,1,512]{2,0,3,1,4:T(2,128)} %copy.6), calls=%async_computation.1 | async-start | bytes 4194304 | tf_op jit(solution)/shard_map/all_to_all | solution.py:50
  240.4 1.8 fusion.49
  242.2 46.0 %all-to-all-done.1 = f32[2,1,512,1,512]{2,0,3,1,4:T(2,128)} async-done(((f32[2,1,512,1,512]{2,0,3,1,4:T(2,128)}), f32[2,1,512,1,512]{2,0,3,1,4:T(2,128)}, u32[]{:S(2)}, u32[]{:S(2)}) %all-to-all-start.1) | async-done | bytes 2097184 | tf_op jit(solution)/shard_map/all_to_all | solution.py:50
  288.2 4.0 %fusion.48 = (f32[1,1,512,1,512]{2,0,3,1,4:T(1,128)S(1)}, f32[1,1,512,1,512]{2,0,3,1,4:T(1,128)S(1)}) fusion(f32[2,1,512,1,512]{2,0,3,1,4:T(2,128)} %all-to-all-done.1), kind=kLoop, calls=%fused_computation.64 | loop fusion | bytes 4194304 | tf_op jit(solution)/shard_map/slice | solution.py:53
  292.2 1.9 fusion.12
  294.1 1.9 fusion.10
  295.9 1.9 fusion.1
  297.8 1.9 fusion
  299.9 3.5 %copy.7 = f32[2,1,512,1,512]{4,3,2,1,0:T(1,128)} copy(f32[2,1,512,1,512]{4,2,0,3,1:T(8,128)S(1)} %maximum_bitcast_fusion.1) | data formatting | bytes 4194304 | tf_op jit(solution)/shard_map/broadcast_in_dim | solution.py:54
  (32 shorter events, 11.9 us)
Async XLA Ops:
  6.5 34.5 %copy-start.4 = (bf16[2,2,1,128,512]{4,3,2,1,0:T(8,128)(2,1)S(1)}, bf16[2,2,1,128,512]{4,3,2,1,0:T(8,128)(2,1)}, u32[]{:S(2)}) copy-start(bf16[2,2,1,128,512]{4,3,2,1,0:T(8,128)(2,1)} %param.5) | copy-start | bytes 1572868
  6.5 33.1 %all-gather.5.cloned.1.call-start = ((), (), s32[]{:S(2)}) async-start(), calls=%async_computation.3 | async-start | bytes 1310720 | tf_op jit(solution)/shard_map/all_gather | solution.py:34
  8.5 60.2 %all-gather.7.cloned.1.call-start = ((), (), s32[]{:S(2)}) async-start(), calls=%async_computation.4 | async-start | bytes 1310720 | tf_op jit(solution)/shard_map/all_gather | solution.py:34
  9.2 119.7 %all-reduce.3.cloned.1.call-start = ((), (), s32[]{:S(2)}) async-start(), calls=%async_computation.5 | async-start | bytes 2097152 | tf_op jit(solution)/shard_map/psum | solution.py:14
  39.6 2.7 copy-start.3
  68.6 2.6 copy-start.2
  130.2 52.0 %copy-start.5 = (f32[2,128,512]{2,1,0:T(8,128)S(1)}, f32[2,128,512]{2,1,0:T(8,128)}, u32[]{:S(2)}) copy-start(f32[2,128,512]{2,1,0:T(8,128)} %get-tuple-element.5) | copy-start | bytes 1572868
  183.8 50.8 %all-to-all-start.2 = ((f32[4,2,128,512]{3,2,1,0:T(8,128)}), f32[4,2,128,512]{3,2,1,0:T(8,128)S(1)}, u32[]{:S(2)}, u32[]{:S(2)}) async-start(f32[4,2,128,512]{3,2,1,0:T(8,128)} %stack.60), calls=%async_computation.2 | async-start | bytes 4194304 | tf_op jit(solution)/shard_map/all_to_all | solution.py:9
  187.4 3.1 %copy-start.1 = (f32[4,2,128,512]{3,2,1,0:T(8,128)S(1)}, f32[4,2,128,512]{3,2,1,0:T(8,128)}, u32[]{:S(2)}) copy-start(f32[4,2,128,512]{3,2,1,0:T(8,128)} %all_to_all.19) | copy-start | bytes 6291460
  234.6 1.3 copy-start
  235.9 52.3 %all-to-all-start.1 = ((f32[2,1,512,1,512]{2,0,3,1,4:T(2,128)}), f32[2,1,512,1,512]{2,0,3,1,4:T(2,128)}, u32[]{:S(2)}, u32[]{:S(2)}) async-start(f32[2,1,512,1,512]{2,0,3,1,4:T(2,128)} %copy.6), calls=%async_computation.1 | async-start | bytes 4194304 | tf_op jit(solution)/shard_map/all_to_all | solution.py:50
Sparse Core Ops, SparseCore 0:
  8.9 30.6 all-gather.4
  41.2 27.3 all-gather.6
  72.7 56.1 all-reduce.2
